TPU v7x, 128 devices: a whole 4x4x4 slice. The times are simulated.
128 devices in a mesh: band: 16 (over x, z_lo, core), grid: 8 (over y, z_hi).
Axes of the slice: x: 4, y: 4, z: 4 (z_hi: 2, z_lo: 2; z = z_hi * 2 + z_lo), core: 2. Of those that a mesh axis runs over, the one named last changes fastest.
Arguments:
- valence: bfloat16 [32, 2, 160, 160, 160], P('band', None, 'grid'), may hold values from -6 to 6
- conduction: bfloat16 [16, 2, 160, 160, 160], P('band', None, 'grid'), may hold values from -6 to 6
- val_energy: float32 [32], replicated, may hold values from -12 to -1
- cond_energy: float32 [16], replicated, may hold values from 1 to 16
- cond_band: int32 [16], P('band'), may hold values from 0 to 15, each once
- owners: int32 [2], replicated, may hold values from 0 to 15
- gvectors: int32 [3, 4096], replicated, may hold values from 0 to 159, as said below
Outputs:
- chi0: float32 [2, 4096, 4096], P(None, 'grid', 'band')
Inputs may be any that keep to these rules, and one draw needn't show every extreme that they name: `gvectors`: the G-vectors are distinct; each component, read between -80 and 80, lies within -10 to 10. `owners`: each entry is an index along band. `cond_band`: A permutation of the global conduction band numbers.
All inputs are finite; a program needn't handle non-finite values.
Results may differ from a plain program's by a relative error of at most 0.0092.
Values may be sent and summed in bfloat16 or wider, within the bound.
No kernel may reach another device: no remote copies, remote signals or barrier semaphores. Data moves between devices by JAX's collectives and lax.ppermute only.
A program may use at most 192 MiB of HBM per device.

v0:
```python
import math

import jax
import jax.numpy as jnp
from jax import lax
from jax.sharding import PartitionSpec as P

ROUNDS = 2


def from_root(block, axis, owner):
    block = jnp.where(lax.axis_index(axis) == owner, block, jnp.zeros_like(block))
    return lax.psum(block, axis)


def dft_tables(length):
    positions = jnp.arange(length, dtype=jnp.int32)
    phase_index = positions[:, None] * positions[None, :] % length
    angles = phase_index.astype(jnp.float32) * (2.0 * math.pi / length)
    return (jnp.cos(angles).astype(jnp.bfloat16), jnp.sin(angles).astype(jnp.bfloat16))


def wide_table(cos_table, sin_table):
    top_half = jnp.concatenate([cos_table, -sin_table], axis=1)
    low_half = jnp.concatenate([sin_table, cos_table], axis=1)
    return jnp.concatenate([top_half, low_half], axis=0)


def plane_transform(density, wide, cos_table, sin_table):
    length = cos_table.shape[0]
    along_z = jnp.einsum("bxyk,kq->bxyq", density, wide, preferred_element_type=jnp.float32).astype(
        jnp.bfloat16
    )
    cos_part = jnp.einsum("bxyk,yq->bxqk", along_z, cos_table, preferred_element_type=jnp.float32)
    sin_part = jnp.einsum("bxyk,yq->bxqk", along_z, sin_table, preferred_element_type=jnp.float32)
    real_part = cos_part[..., :length] + sin_part[..., length:]
    imag_part = cos_part[..., length:] - sin_part[..., :length]
    return jnp.concatenate([real_part, imag_part], axis=-1).astype(jnp.bfloat16)


def shards(valence, conduction, val_energy, cond_energy, cond_band, owners, gvectors):
    val_dev = valence.shape[0]
    cond_dev = conduction.shape[0]
    x_local = valence.shape[2]
    length = valence.shape[3]
    y_local = length // lax.axis_size("grid")
    grid_pos = lax.axis_index("grid")
    band_pos = lax.axis_index("band")
    cos_table, sin_table = dft_tables(length)
    wide = wide_table(cos_table, sin_table)
    freq_x, freq_y, freq_z = (gvectors[0], gvectors[1], gvectors[2])
    norm_factor = float(length) ** (-1.5)
    pairs_all = ROUNDS * val_dev * cond_dev * lax.axis_size("band")
    cond_numbers = jnp.arange(cond_energy.shape[0], dtype=jnp.int32)
    cond_levels = jnp.sum(
        jnp.where(cond_band[:, None] == cond_numbers[None, :], cond_energy[None, :], 0.0), axis=1
    )
    cond_f = conduction.astype(jnp.float32)[None]
    local_y = freq_y - grid_pos * y_local
    inside = (local_y >= 0) & (local_y < y_local)
    local_y = jnp.clip(local_y, 0, y_local - 1)
    elem_rounds = []
    weight_rounds = []
    for round_no in range(ROUNDS):
        owner_pos = owners[round_no]
        val_bands = from_root(valence, "band", owner_pos)
        val_levels = lax.dynamic_slice_in_dim(val_energy, owner_pos * val_dev, val_dev, 0)
        val_f = val_bands.astype(jnp.float32)[:, None]
        dens_re = val_f[:, :, 0] * cond_f[:, :, 0] + val_f[:, :, 1] * cond_f[:, :, 1]
        dens_im = val_f[:, :, 0] * cond_f[:, :, 1] - val_f[:, :, 1] * cond_f[:, :, 0]
        density = jnp.concatenate([dens_re, dens_im], axis=-1).astype(jnp.bfloat16)
        density = density.reshape(val_dev * cond_dev, x_local, length, 2 * length)
        plane = plane_transform(density, wide, cos_table, sin_table)
        block = lax.all_to_all(plane, "grid", split_axis=2, concat_axis=1, tiled=True)
        cos_part = jnp.einsum("bxyk,xq->bqyk", block, cos_table, preferred_element_type=jnp.float32)
        sin_part = jnp.einsum("bxyk,xq->bqyk", block, sin_table, preferred_element_type=jnp.float32)
        full_re = cos_part[..., :length] + sin_part[..., length:]
        full_im = cos_part[..., length:] - sin_part[..., :length]
        elem_re = jnp.where(inside[None, :], full_re[:, freq_x, local_y, freq_z], 0.0) * norm_factor
        elem_im = jnp.where(inside[None, :], full_im[:, freq_x, local_y, freq_z], 0.0) * norm_factor
        elem_round = jnp.stack([elem_re, elem_im], axis=1)
        elem_rounds.append(elem_round)
        pair_weight = 2.0 / (pairs_all * (val_levels[:, None] - cond_levels[None, :]))
        weight_rounds.append(pair_weight.reshape(val_dev * cond_dev))
    local_elements = jnp.concatenate(elem_rounds, axis=0)
    local_weights = jnp.concatenate(weight_rounds, axis=0)
    summed = lax.psum(local_elements, "grid")
    row_count = summed.shape[2] // lax.axis_size("grid")
    col_count = summed.shape[2] // lax.axis_size("band")
    gathered, all_weights = (
        lax.all_gather(summed, "band", axis=0, tiled=True),
        lax.all_gather(local_weights, "band", axis=0, tiled=True),
    )
    row_block = lax.dynamic_slice_in_dim(gathered, grid_pos * row_count, row_count, 2)
    col_block = lax.dynamic_slice_in_dim(gathered, band_pos * col_count, col_count, 2)
    weighted = row_block * all_weights[:, None, None]
    right_side = jnp.concatenate([col_block[:, 0], col_block[:, 1]], axis=0)
    left_real = jnp.concatenate([weighted[:, 0], weighted[:, 1]], axis=0)
    left_imag = jnp.concatenate([weighted[:, 1], -weighted[:, 0]], axis=0)
    high = lax.Precision.HIGHEST
    chi_re = jnp.einsum("pr,pc->rc", left_real, right_side, precision=high)
    chi_im = jnp.einsum("pr,pc->rc", left_imag, right_side, precision=high)
    return jnp.stack([chi_re, chi_im])


def solution(mesh):
    return jax.shard_map(
        shards,
        mesh=mesh,
        in_specs=(
            P("band", None, "grid", None, None),
            P("band", None, "grid", None, None),
            P(),
            P(),
            P("band"),
            P(),
            P(),
        ),
        out_specs=P(None, "grid", "band"),
        check_vma=False,
    )
```

profile of v0, /device:TPU:38, one launch (start us, length us, event | category | flops | bytes accessed | tf_op | source)
XLA Modules:
  0.0 952.0 jit_solution(14158442999222053255)
XLA Ops:
  9.2 8.4 select_bitcast_fusion.1
  22.5 285.1 %all-reduce.7.cloned.1.call-done = (bf16[2,1,2,20,160,160]{5,4,3,0,2,1:T(8,128)(2,1)}, bf16[2,1,2,20,160,160]{5,4,3,0,2,1:T(8,128)(2,1)}) async-done(((bf16[2,1,2,20,160,160]{5,4,3,0,2,1:T(8,128)(2,1)}, bf16[2,1,2,20,160,160]{5,4,3,0,2,1:T(8,128)(2,1)}), (bf16[2,1,2,20,160,160]{5,4,3,0,2,1:T(8,128)(2,1)}, bf16[2,1,2,20,160,160]{5,4,3,0,2,1:T(8,128)(2,1)})) %all-reduce.7.cloned.1.call-update) | async-done | bytes 8192016 | tf_op jit(solution)/shard_map/psum | solution.py:13
  307.6 9.6 %broadcast_in_dim.74 = f32[2,1,2,20,160,160]{5,4,3,0,2,1:T(8,128)} convert(bf16[2,1,2,20,160,160]{5,4,3,0,2,1:T(8,128)(2,1)} %get-tuple-element.6) | non-fusion elementwise | flops 2048000 | bytes 12288000 | tf_op jit(solution)/shard_map/broadcast_in_dim | solution.py:68
  323.9 16.5 %add_convert_fusion.1 = (bf16[2,20,160,160]{3,2,1,0:T(8,128)(2,1)}, bf16[2,20,160,160]{3,2,1,0:T(8,128)(2,1)}, bf16[2,20,160,160]{3,2,1,0:T(8,128)(2,1)}, bf16[2,20,160,160]{3,2,1,0:T(8,128)(2,1)}) fusion(f32[2,1,2,20,160,160]{5,4,3,0,2,1:T(8,128)} %broadcast_in_dim.74, f32[20,160,160]{2,1,0:T(8,128)} %get-tuple-element.22, ...), kind=kLoop, calls=%fused_computation.24 | loop fusion | flops 16384000 | bytes 28672000 | tf_op jit(solution)/shard_map/convert.9
  368.3 9.7 %copy.88 = bf16[2,20,160,320]{3,0,1,2:T(2,128)(2,1)} copy(bf16[2,20,160,320]{3,2,1,0:T(8,128)(2,1)} %pad_maximum_fusion.1) | data formatting | bytes 8192000 | tf_op jit(solution)/shard_map/concatenate | solution.py:38
  411.7 9.7 %copy.76 = bf16[2,20,160,320]{3,0,1,2:T(2,128)(2,1)} copy(bf16[2,20,160,320]{3,2,1,0:T(8,128)(2,1)} %pad_maximum_fusion) | data formatting | bytes 8192000 | tf_op jit(solution)/shard_map/concatenate | solution.py:38
  421.5 28.7 %all-to-all-done.1 = bf16[2,20,160,320]{3,0,1,2:T(2,128)(2,1)} async-done(((bf16[2,20,160,320]{3,0,1,2:T(2,128)(2,1)}), bf16[2,20,160,320]{3,0,1,2:T(2,128)(2,1)}, u32[]{:S(2)}, u32[]{:S(2)}) %all-to-all-start.1) | async-done | bytes 4096032 | tf_op jit(solution)/shard_map/all_to_all | solution.py:74
  455.5 7.9 copy.90
  463.4 8.3 fusion.26
  477.5 44.2 %all-to-all-done = bf16[2,20,160,320]{3,0,1,2:T(2,128)(2,1)} async-done(((bf16[2,20,160,320]{3,0,1,2:T(2,128)(2,1)}), bf16[2,20,160,320]{3,0,1,2:T(2,128)(2,1)}, u32[]{:S(2)}, u32[]{:S(2)}) %all-to-all-start) | async-done | bytes 4096032 | tf_op jit(solution)/shard_map/all_to_all | solution.py:74
  521.8 8.0 copy.78
  529.8 8.7 fusion.20
  544.3 9.4 slice_add_fusion
  553.7 10.7 %copy.96 = f32[2,160,20,160]{3,0,2,1:T(2,128)} copy(f32[2,160,20,160]{3,1,2,0:T(8,128)} %get-tuple-element.14) | data formatting | bytes 8192000 | tf_op jit(solution)/shard_map/sub | solution.py:78
  564.4 10.6 %copy.95 = f32[2,160,20,160]{3,0,2,1:T(2,128)} copy(f32[2,160,20,160]{3,1,2,0:T(8,128)} %get-tuple-element.13) | data formatting | bytes 8192000 | tf_op jit(solution)/shard_map/add | solution.py:77
  575.0 51.4 %gather_fusion.3 = f32[4096,2]{0,1:T(2,128)S(1)} fusion(f32[2,160,20,160]{3,0,2,1:T(2,128)} %copy.96, s32[4096]{0:T(1024)S(1)} %bitcast.147), kind=kCustom, calls=%fused_computation.3 | custom fusion | bytes 114688 | tf_op jit(solution)/shard_map/gather | solution.py:80
  626.4 51.5 %gather_fusion.2 = f32[4096,2]{0,1:T(2,128)S(1)} fusion(f32[2,160,20,160]{3,0,2,1:T(2,128)} %copy.95, s32[4096]{0:T(1024)S(1)} %bitcast.148), kind=kCustom, calls=%fused_computation.2 | custom fusion | bytes 114688 | tf_op jit(solution)/shard_map/gather | solution.py:79
  677.8 15.4 %slice_add_fusion.2 = (f32[2,160,20,160]{3,1,2,0:T(8,128)}, f32[2,160,20,160]{3,1,2,0:T(8,128)}) fusion(f32[2,160,20,320]{3,1,2,0:T(8,128)} %fusion.23, f32[2,160,20,320]{3,1,2,0:T(8,128)} %fusion.20), kind=kLoop, calls=%fused_computation.13 | loop fusion | flops 2048000 | bytes 24576000 | tf_op jit(solution)/shard_map/add | solution.py:77
  693.3 10.7 %copy.84 = f32[2,160,20,160]{3,0,2,1:T(2,128)} copy(f32[2,160,20,160]{3,1,2,0:T(8,128)} %get-tuple-element.8) | data formatting | bytes 8192000 | tf_op jit(solution)/shard_map/sub | solution.py:78
  703.9 51.4 %gather_fusion.1 = f32[4096,2]{0,1:T(2,128)S(1)} fusion(f32[2,160,20,160]{3,0,2,1:T(2,128)} %copy.84, s32[4096]{0:T(1024)S(1)} %bitcast.149), kind=kCustom, calls=%fused_computation.1 | custom fusion | bytes 114688 | tf_op jit(solution)/shard_map/gather | solution.py:80
  755.4 10.7 %copy.83 = f32[2,160,20,160]{3,0,2,1:T(2,128)} copy(f32[2,160,20,160]{3,1,2,0:T(8,128)} %get-tuple-element.7) | data formatting | bytes 8192000 | tf_op jit(solution)/shard_map/add | solution.py:77
  766.0 51.2 %gather_fusion = f32[4096,2]{0,1:T(2,128)S(1)} fusion(f32[2,160,20,160]{3,0,2,1:T(2,128)} %copy.83, s32[4096]{0:T(1024)S(1)} %bitcast.150), kind=kCustom, calls=%fused_computation | custom fusion | bytes 114688 | tf_op jit(solution)/shard_map/gather | solution.py:79
  818.1 89.4 %all-reduce.5.cloned.1.call-done = f32[4,2,4096]{2,0,1:T(4,128)} async-done(((f32[4,2,4096]{2,0,1:T(4,128)}), f32[4,2,4096]{2,0,1:T(4,128)}) %all-reduce.5.cloned.1.call-update) | async-done | bytes 131088 | tf_op jit(solution)/shard_map/psum | solution.py:87
  913.9 23.8 %all-reduce = f32[64]{0:T(128)S(1)} all-reduce(f32[64]{0:T(128)S(1)} %maximum_dynamic-update-slice_fusion), channel_id=1, replica_groups=mesh['band'=16,'grid'=8] {'band'}, use_global_device_ids=true, to_apply=%add | all-reduce | flops 64 | bytes 512
  (77 shorter events, 103.4 us)
Async XLA Ops:
  6.5 301.1 %all-reduce.7.cloned.1.call-start = ((), (), s32[]{:S(2)}) async-start(), calls=%async_computation.4 | async-start | bytes 26214400 | tf_op jit(solution)/shard_map/psum | solution.py:13
  17.6 1.9 copy-start.6
  307.6 9.6 %copy-start.4 = (bf16[2,1,2,20,160,160]{5,4,3,0,2,1:T(8,128)(2,1)S(1)}, bf16[2,1,2,20,160,160]{5,4,3,0,2,1:T(8,128)(2,1)}, u32[]{:S(2)}) copy-start(bf16[2,1,2,20,160,160]{5,4,3,0,2,1:T(8,128)(2,1)} %get-tuple-element.5) | copy-start | bytes 12288004
  346.6 2.2 copy-start.3
  378.0 6.7 copy-start.5
  378.0 72.1 %all-to-all-start.1 = ((bf16[2,20,160,320]{3,0,1,2:T(2,128)(2,1)}), bf16[2,20,160,320]{3,0,1,2:T(2,128)(2,1)}, u32[]{:S(2)}, u32[]{:S(2)}) async-start(bf16[2,20,160,320]{3,0,1,2:T(2,128)(2,1)} %copy.88), calls=%async_computation.1 | async-start | bytes 9830400 | tf_op jit(solution)/shard_map/all_to_all | solution.py:74
  390.0 2.3 copy-start.2
  421.5 33.8 %copy-start.7 = (s32[3,4096]{1,0:T(4,128)S(1)}, s32[3,4096]{1,0:T(4,128)}, u32[]{:S(2)}) copy-start(s32[3,4096]{1,0:T(4,128)} %param.13) | copy-start | bytes 147460
  450.1 71.6 %all-to-all-start = ((bf16[2,20,160,320]{3,0,1,2:T(2,128)(2,1)}), bf16[2,20,160,320]{3,0,1,2:T(2,128)(2,1)}, u32[]{:S(2)}, u32[]{:S(2)}) async-start(bf16[2,20,160,320]{3,0,1,2:T(2,128)(2,1)} %copy.76), calls=%async_computation | async-start | bytes 9830400 | tf_op jit(solution)/shard_map/all_to_all | solution.py:74
  454.8 452.7 %all-reduce.5.cloned.1.call-start = ((), (), s32[]{:S(2)}) async-start(), calls=%async_computation.2 | async-start | bytes 262144 | tf_op jit(solution)/shard_map/psum | solution.py:87
  463.4 8.3 copy-start
  529.8 8.7 copy-start.1
  529.8 14.5 %slice-start = ((s8[9830400]{0:T(1024)(128)(4,1)}), s8[4194304]{0:T(1024)(128)(4,1)S(1)}, s32[]{:S(2)}) async-start(s8[9830400]{0:T(1024)(128)(4,1)} %bitcast.151), calls=%async_computation.5 | async-start | bytes 8388608
  529.8 14.5 %slice-start.1 = ((s8[9830400]{0:T(1024)(128)(4,1)}), s8[4194304]{0:T(1024)(128)(4,1)S(1)}, s32[]{:S(2)}) async-start(s8[9830400]{0:T(1024)(128)(4,1)} %bitcast.151), calls=%async_computation.6 | async-start | bytes 8388608
  538.5 5.8 slice-start.2
  766.0 145.1 %copy-start.10 = (u32[128]{0:T(128)S(1)}, u32[128]{0:T(128)}, u32[]{:S(2)}) copy-start(u32[128]{0:T(128)} %constant.132) | copy-start | bytes 1540
  766.0 146.4 %copy-start.9 = (f32[16]{0:T(128)S(1)}, f32[16]{0:T(128)}, u32[]{:S(2)}) copy-start(f32[16]{0:T(128)} %param.10) | copy-start | bytes 196
  766.0 147.0 %copy-start.8 = (f32[32]{0:T(128)S(1)}, f32[32]{0:T(128)}, u32[]{:S(2)}) copy-start(f32[32]{0:T(128)} %param.9) | copy-start | bytes 388
  818.0 122.1 %all-gather.2.cloned.1.call-start = ((), (), s32[]{:S(2)}) async-start(), calls=%async_computation.3 | async-start | bytes 2228224 | tf_op jit(solution)/shard_map/all_gather | solution.py:91
Sparse Core Ops, SparseCore 0:
  17.8 289.7 all-reduce.6
  818.2 89.2 all-reduce.4
  909.3 30.7 all-gather.1
where the time goes:
time: 963 us; the launch traced here: 952 us
  waiting for transfers between devices  450 us (47%)
  local copies, waits for them, and re-layouts  296 us (31%)
  other arithmetic  98.7 us (10%)
  matrix products  54.4 us (6%)
  blocking collectives  23.8 us (2%)
  between operations  17.7 us (2%)
  starting transfers between devices  11.8 us (1%)
    psum x1, waiting for transfers between devices, from_root(): return lax.psum(block, axis)  285 us
    gather x2, local copies, waits for them, and re-layouts, shards(): full_im[:, freq_x, local_y, freq_z]  103 us
    gather x2, local copies, waits for them, and re-layouts, shards(): full_re[:, freq_x, local_y, freq_z]  103 us
    psum x1, waiting for transfers between devices, shards(): summed = lax.psum(local_elements, 'grid')  89.4 us
    all_to_all x2, waiting for transfers between devices, shards(): lax.all_to_all(plane, 'grid', split_axis=2, concat_axis=1, tiled=True)  72.9 us
    another operation x3, other arithmetic  28.6 us
    add x2, other arithmetic, shards(): full_re = cos_part[..., :length] + sin_part[..., length:]  24.8 us
    broadcast_in_dim x3, other arithmetic, shards(): val_f = val_bands.astype(jnp.float32)[:, None]  24.7 us
  transfers between devices with their start and end apart: 5, of which 5 were waited for; matrix products, arithmetic and copies ran while one was open for 7% of the time, Pallas kernels for 0%

commit v1 on v0

v1 whole, which is shorter than its diff:
```python
import functools
import math

import jax
import jax.numpy as jnp
import numpy as np
from jax import lax
from jax.experimental import pallas as pl
from jax.experimental.pallas import tpu as pltpu
from jax.sharding import PartitionSpec as P

LENGTH = 160
GMAX = 10
SIDE = 2 * GMAX + 1
PARTS = 16
ROWS = 200
TAIL = 104
WIRE = 2 * ROWS + TAIL
PAIRS = 64
KROWS = 24
GCHUNK = 256
BF = jnp.bfloat16
F32 = jnp.float32


def host_tables():
    freq = (np.arange(SIDE) - GMAX) % LENGTH
    pos = np.arange(LENGTH)
    angle = ((freq[:, None] * pos[None, :]) % LENGTH).astype(np.float32) * np.float32(2.0 * math.pi / LENGTH)
    rnd = lambda a: a.astype(np.float32).astype(jnp.bfloat16).astype(np.float32)
    return rnd(np.cos(angle)), rnd(np.sin(angle))


def z_table():
    cos, sin = host_tables()
    out = np.zeros((2 * KROWS, 384), np.float32)
    cm, sm, ct, st = cos[:, :128], sin[:, :128], cos[:, 128:], sin[:, 128:]
    out[:SIDE] = np.concatenate([cm, sm, ct, ct, st, -st], axis=1)
    out[KROWS : KROWS + SIDE] = np.concatenate([-sm, cm, -st, -st, ct, -ct], axis=1)
    return out.astype(jnp.bfloat16)


def y_tables():
    cos, sin = host_tables()
    out = np.zeros((4, 256, 4, 32), np.float32)
    for shift in range(4):
        for row in range(ROWS):
            flat = 40 * shift + row
            x, y = divmod(flat, LENGTH)
            out[shift, row, 2 * x, :SIDE] = cos[:, y]
            out[shift, row, 2 * x + 1, :SIDE] = sin[:, y]
    return out.reshape(4, 256, 128).astype(jnp.bfloat16)


def pack_kernel(number_ref, cond_ref, val_ref, out_ref):
    number = number_ref[0].astype(F32)
    for band in range(3):
        src = cond_ref if band == 0 else val_ref.at[band - 1]
        real, imag = src[0], src[1]
        out_ref[0, band, 0:ROWS] = real[:, :128]
        out_ref[0, band, ROWS : 2 * ROWS] = imag[:, :128]
        tail = jnp.concatenate([real[:, 128:].astype(F32), imag[:, 128:].astype(F32)], axis=1)
        low = tail[:TAIL]
        fill = jnp.full((2 * TAIL - ROWS, 64), 1.0, F32) * number
        high = jnp.concatenate([tail[TAIL:], fill], axis=0)
        out_ref[0, band, 2 * ROWS :] = jnp.concatenate([low, high], axis=1).astype(BF)


def pack(conduction, valence, number):
    return pl.pallas_call(
        pack_kernel,
        out_shape=jax.ShapeDtypeStruct((PARTS, 3, WIRE, 128), BF),
        grid_spec=pltpu.PrefetchScalarGridSpec(
            num_scalar_prefetch=1,
            grid=(PARTS,),
            in_specs=[
                pl.BlockSpec((2, ROWS, LENGTH), lambda t, n: (0, t, 0)),
                pl.BlockSpec((2, 2, ROWS, LENGTH), lambda t, n: (0, 0, t, 0)),
            ],
            out_specs=pl.BlockSpec((1, 3, WIRE, 128), lambda t, n: (t, 0, 0, 0)),
        ),
        name="pack",
    )(number, conduction, valence)


def unpack_tail(tail):
    return jnp.concatenate([tail[:, :64], tail[: ROWS - TAIL, 64:]], axis=0)


def z_kernel(own_ref, v0_ref, v1_ref, cond_ref, table_ref, out_ref, val_main, val_tail, low_ref, high_ref):
    step = pl.program_id(0)

    @pl.when(step == 0)
    def _():
        for i in range(4):
            src = (v0_ref if i < 2 else v1_ref).at[0, 1 + i % 2]
            val_main[i, 0] = src[0:ROWS].astype(F32)
            val_main[i, 1] = src[ROWS : 2 * ROWS].astype(F32)
            both = unpack_tail(src[2 * ROWS :].astype(F32))
            val_tail[i] = jnp.concatenate([both, both], axis=1)
        high_ref[...] = jnp.zeros_like(high_ref)

    cre = cond_ref[0, 0, 0:ROWS].astype(F32)
    cim = cond_ref[0, 0, ROWS : 2 * ROWS].astype(F32)
    both = unpack_tail(cond_ref[0, 0, 2 * ROWS :].astype(F32))
    ctail = jnp.concatenate([both, both[:, 32:], both[:, :32]], axis=1)
    for i in range(4):
        vre, vim = val_main[i, 0], val_main[i, 1]
        dre = vre * cre + vim * cim
        dim = vre * cim - vim * cre
        tail = val_tail[i] * ctail
        density = jnp.concatenate([dre, dim, tail], axis=1).astype(BF)
        along = lax.dot_general(
            table_ref[...], density, (((1,), (1,)), ((), ())), preferred_element_type=F32
        )
        for part in range(2):
            start = part * PAIRS + step * 4 + i
            piece = along[part * KROWS : (part + 1) * KROWS]
            low_ref[pl.ds(start, KROWS, stride=128), :] = piece[:, :128]
            high_ref[pl.ds(start, KROWS, stride=128), 0 : ROWS - 128] = piece[:, 128:]

    @pl.when(step == pl.num_programs(0) - 1)
    def _():
        out_ref[:, :128] = low_ref[...].astype(BF)
        out_ref[:, 128:] = high_ref[...].astype(BF)


def z_transform(wire, owners):
    return pl.pallas_call(
        z_kernel,
        out_shape=jax.ShapeDtypeStruct((KROWS * 128, 256), BF),
        grid_spec=pltpu.PrefetchScalarGridSpec(
            num_scalar_prefetch=1,
            grid=(PARTS,),
            in_specs=[
                pl.BlockSpec((1, 3, WIRE, 128), lambda c, o: (o[0], 0, 0, 0)),
                pl.BlockSpec((1, 3, WIRE, 128), lambda c, o: (o[1], 0, 0, 0)),
                pl.BlockSpec((1, 1, WIRE, 128), lambda c, o: (c, 0, 0, 0)),
                pl.BlockSpec((2 * KROWS, 384), lambda c, o: (0, 0)),
            ],
            out_specs=pl.BlockSpec((KROWS * 128, 256), lambda c, o: (0, 0)),
            scratch_shapes=[
                pltpu.VMEM((4, 2, ROWS, 128), F32),
                pltpu.VMEM((4, ROWS, 128), F32),
                pltpu.VMEM((KROWS * 128, 128), F32),
                pltpu.VMEM((KROWS * 128, 128), F32),
            ],
        ),
        compiler_params=pltpu.CompilerParams(vmem_limit_bytes=40 * 2**20),
        name="ztransform",
    )(owners, wire, wire, wire, jnp.asarray(z_table()))


def g_kernel(along_ref, ytab_ref, index_ref, phase_ref, out_ref, plane_ref):
    @pl.when(pl.program_id(0) == 0)
    def _():
        lane = lax.broadcasted_iota(jnp.int32, (256, 256), 1) // 32
        for tile in range(3):
            parts = [None] * 4
            for s in range(8):
                k = tile * 8 + s
                if k >= SIDE:
                    continue
                left = along_ref[k * 128 : (k + 1) * 128]
                for t in range(4):
                    right = jnp.where(lane == s, ytab_ref[t], jnp.zeros((256, 256), BF))
                    term = jnp.dot(left, right, preferred_element_type=F32)
                    parts[t] = term if parts[t] is None else parts[t] + term
            for x in range(2):
                c, s = parts[2 * x], parts[2 * x + 1]
                real = c[:PAIRS] + s[PAIRS:]
                imag = c[PAIRS:] - s[:PAIRS]
                block = jnp.concatenate([real, imag], axis=0)
                plane_ref[x, :, tile * 256 : (tile + 1) * 256] = block.astype(BF)

    row = lax.broadcasted_iota(jnp.int32, (768, GCHUNK), 0)
    pick = jnp.where(row == index_ref[0], 1.0, 0.0).astype(BF)
    real = jnp.zeros((PAIRS, GCHUNK), F32)
    imag = jnp.zeros((PAIRS, GCHUNK), F32)
    for x in range(2):
        at = jnp.dot(plane_ref[x], pick, preferred_element_type=F32)
        c = phase_ref[0, 2 * x : 2 * x + 1]
        s = phase_ref[0, 2 * x + 1 : 2 * x + 2]
        real = real + at[:PAIRS] * c + at[PAIRS:] * s
        imag = imag + at[PAIRS:] * c - at[:PAIRS] * s
    out_ref[0, :PAIRS] = real.astype(BF)
    out_ref[0, PAIRS:] = imag.astype(BF)


def g_elements(along, ytab, index, phase):
    chunks = index.shape[0]
    return pl.pallas_call(
        g_kernel,
        out_shape=jax.ShapeDtypeStruct((chunks, 128, GCHUNK), BF),
        grid=(chunks,),
        in_specs=[
            pl.BlockSpec((KROWS * 128, 256), lambda i: (0, 0)),
            pl.BlockSpec((4, 256, 256), lambda i: (0, 0, 0)),
            pl.BlockSpec((1, 1, GCHUNK), lambda i: (i, 0, 0)),
            pl.BlockSpec((1, 4, GCHUNK), lambda i: (i, 0, 0)),
        ],
        out_specs=pl.BlockSpec((1, 128, GCHUNK), lambda i: (i, 0, 0)),
        scratch_shapes=[pltpu.VMEM((2, 128, 768), BF)],
        compiler_params=pltpu.CompilerParams(vmem_limit_bytes=40 * 2**20),
        name="gelements",
    )(along, ytab, index, phase)


def shards(valence, conduction, val_energy, cond_energy, cond_band, owners, gvectors):
    grid_pos = lax.axis_index("grid")
    band_pos = lax.axis_index("band")
    x_local = valence.shape[2]
    n_grid = lax.axis_size("grid")

    wire = pack(
        conduction.reshape(2, x_local * LENGTH, LENGTH),
        valence.reshape(2, 2, x_local * LENGTH, LENGTH),
        cond_band,
    )
    wire = lax.all_to_all(wire, "band", 0, 0, tiled=True)

    numbers = wire[:, 0, WIRE - 1, 127].astype(jnp.int32)
    order = jnp.arange(cond_energy.shape[0], dtype=jnp.int32)
    levels = jnp.sum(jnp.where(numbers[:, None] == order[None, :], cond_energy[None, :], 0.0), axis=1)
    val_index = (owners[:, None] * 2 + jnp.arange(2, dtype=jnp.int32)[None, :]).reshape(4)
    val_levels = val_energy[val_index]
    weight = (2.0 / (PAIRS * (val_levels[None, :] - levels[:, None]))).reshape(PAIRS)

    along = z_transform(wire, owners)

    ytab = lax.dynamic_index_in_dim(jnp.asarray(y_tables()), band_pos % 4, 0, keepdims=False)
    ytab = jnp.tile(ytab.reshape(256, 4, 32).transpose(1, 0, 2), (1, 1, 8))
    signed = (gvectors + GMAX) % LENGTH
    index = (signed[2] * 32 + signed[1]).reshape(PARTS, 1, GCHUNK)
    x_first = grid_pos * x_local + 5 * (band_pos // 4) + band_pos % 4
    norm = float(LENGTH) ** (-1.5)
    waves = []
    for x in range(2):
        angle = (gvectors[0] * (x_first + x) % LENGTH).astype(F32) * (2.0 * math.pi / LENGTH)
        waves += [jnp.cos(angle), jnp.sin(angle)]
    phase = jnp.stack(waves).astype(BF).astype(F32) * norm
    phase = phase.reshape(4, PARTS, GCHUNK).transpose(1, 0, 2)
    parts = g_elements(along, ytab, index, phase)

    parts = lax.all_to_all(parts, "band", 0, 0, tiled=True)
    block = jnp.sum(parts.astype(F32), axis=0)
    zh_flip = [(g, g ^ 1) for g in range(n_grid)]
    y_flip = [(g, g ^ 2) for g in range(n_grid)]
    y_rest = [(g, 6 - (g & 6) + (g & 1)) for g in range(n_grid)]
    for perm in (zh_flip, y_flip, y_rest):
        block = block + lax.ppermute(block, "grid", perm)

    straight, crossed = [], []
    for b in range(PARTS):
        for g in range(n_grid):
            straight.append((b * n_grid + g, (2 * g + b % 2) * n_grid + b // 2))
            crossed.append((b * n_grid + g, (2 * g + 1 - b % 2) * n_grid + b // 2))
    same = lax.ppermute(block, ("band", "grid"), straight)
    other = lax.ppermute(block, ("band", "grid"), crossed)
    odd = (band_pos % 2) == 1
    first = jnp.where(odd, other, same)
    second = jnp.where(odd, same, other)
    rows = jnp.concatenate([first, second], axis=1)

    w2 = jnp.concatenate([weight, weight])[:, None]
    for_real = block * w2
    for_imag = jnp.concatenate([-for_real[PAIRS:], for_real[:PAIRS]], axis=0)
    high = lax.Precision.HIGHEST
    chi_re = jnp.einsum("pr,pc->rc", rows, for_real, precision=high)
    chi_im = jnp.einsum("pr,pc->rc", rows, for_imag, precision=high)
    return jnp.stack([chi_re, chi_im])


def solution(mesh):
    return jax.shard_map(
        shards,
        mesh=mesh,
        in_specs=(
            P("band", None, "grid", None, None),
            P("band", None, "grid", None, None),
            P(),
            P(),
            P("band"),
            P(),
            P(),
        ),
        out_specs=P(None, "grid", "band"),
        check_vma=False,
    )
```

time: 963 us -> 197 us (0.20)
  the two profiles are of different devices: /device:TPU:38 before, /device:TPU:7 now
where the time goes in v1:
time: 197 us; the launch traced here: 196 us
  waiting for transfers between devices  119 us (60%)
  Pallas kernels  35.5 us (18%)
  starting transfers between devices  31.9 us (16%)
  other arithmetic  5.01 us (3%)
    all_to_all x1, waiting for transfers between devices, shards(): wire = lax.all_to_all(wire, 'band', 0, 0, tiled=True)  90.4 us
    all_to_all x1, waiting for transfers between devices, shards(): parts = lax.all_to_all(parts, 'band', 0, 0, tiled=True)  13.6 us
    pallas_call x1, Pallas kernels, z_transform(): pl.pallas_call(z_kernel, out_shape=jax.ShapeDtypeStruct((KROWS * 128, 256...  13.2 us
    pallas_call x1, Pallas kernels, pack(): pl.pallas_call(pack_kernel, out_shape=jax.ShapeDtypeStruct((PARTS, 3, WIR...  13 us
    pallas_call x1, Pallas kernels, g_elements(): pl.pallas_call(g_kernel, out_shape=jax.ShapeDtypeStruct((chunks, 128, GCH...  9.37 us
    ppermute x1, starting transfers between devices, shards(): other = lax.ppermute(block, ('band', 'grid'), crossed)  8.11 us
    ppermute x3, starting transfers between devices, shards(): block = block + lax.ppermute(block, 'grid', perm)  7.57 us
    all_to_all x1, starting transfers between devices, shards(): parts = lax.all_to_all(parts, 'band', 0, 0, tiled=True)  7.43 us
  transfers between devices with their start and end apart: 7, of which 7 were waited for; matrix products, arithmetic and copies ran while one was open for 3% of the time, Pallas kernels for 0%

profile of v1, /device:TPU:7, one launch (start us, length us, event | category | flops | bytes accessed | tf_op | source)
XLA Modules:
  0.0 195.9 jit_solution(12467534369834219366)
XLA Ops:
  0.7 13.0 %pack.1 = bf16[16,3,504,128]{3,2,1,0:T(8,128)(2,1)} custom-call(s32[1]{0:T(128)S(6)} %copy.12.number_ref, bf16[2,3200,160]{2,1,0:T(8,128)(2,1)} %bitcast.22, bf16[2,2,3200,160]{3,2,1,0:T(8,128)(2,1)} %bitcast.21), custom_call_target="tpu_custom_call" | custom-call | tf_op jit(solution)/shard_map/pack/pallas_call | solution.py:70
  13.6 6.6 %all-to-all-start = ((bf16[16,3,504,128]{3,2,1,0:T(8,128)(2,1)}), bf16[16,3,504,128]{3,2,1,0:T(8,128)(2,1)}, u32[]{:S(2)}, u32[]{:S(2)}) async-start(bf16[16,3,504,128]{3,2,1,0:T(8,128)(2,1)} %pack.1), calls=%async_computation | async-start | bytes 12386304 | tf_op jit(solution)/shard_map/all_to_all | solution.py:220
  20.2 0.8 constant_dynamic-slice_fusion
  21.4 1.0 cosine_convert_fusion.1
  22.4 0.9 sine_convert_fusion
  23.5 90.4 %all-to-all-done.v0_ref.v1_ref.cond_ref = bf16[16,3,504,128]{3,2,1,0:T(8,128)(2,1)} async-done(((bf16[16,3,504,128]{3,2,1,0:T(8,128)(2,1)}), bf16[16,3,504,128]{3,2,1,0:T(8,128)(2,1)}, u32[]{:S(2)}, u32[]{:S(2)}) %all-to-all-start) | async-done | bytes 6193184 | tf_op jit(solution)/shard_map/all_to_all | solution.py:220
  113.9 13.2 %ztransform.1.along_ref = bf16[3072,256]{1,0:T(8,128)(2,1)S(1)} custom-call(s32[2]{0:T(128)S(1)} %copy-done.2, bf16[16,3,504,128]{3,2,1,0:T(8,128)(2,1)} %all-to-all-done.v0_ref.v1_ref.cond_ref, bf16[16,3,504,128]{3,2,1,0:T(8,128)(2,1)} %all-to-all-done.v0_ref.v1_ref.cond_ref, bf16[16,3,504,128]{3,2,1,0:T(8,128)(2,1)} %all-to-all-done.v0_ref.v1_ref.cond_ref, ...), custom_call_target="tpu_custom_call" | custom-call | tf_op jit(solution)/shard_map/ztransform/pallas_call | solution.py:129
  127.1 9.4 %gelements.1 = bf16[16,128,256]{2,1,0:T(8,128)(2,1)} custom-call(bf16[3072,256]{1,0:T(8,128)(2,1)S(1)} %ztransform.1.along_ref, bf16[4,256,256]{2,1,0:T(8,128)(2,1)S(1)} %copy.11.ytab_ref, s32[16,1,256]{2,1,0:T(1,128)S(1)} %bitcast.20, f32[16,4,256]{2,1,0:T(4,128)S(1)} %multiply_bitcast_fusion.phase_ref), custom_call_target="tpu_custom_call" | custom-call | tf_op jit(solution)/shard_map/gelements/pallas_call | solution.py:192
  136.5 7.4 %all-to-all-start.1 = ((bf16[16,128,256]{2,1,0:T(8,128)(2,1)}), bf16[16,128,256]{2,1,0:T(8,128)(2,1)S(1)}, u32[]{:S(2)}, u32[]{:S(2)}) async-start(bf16[16,128,256]{2,1,0:T(8,128)(2,1)} %gelements.1), calls=%async_computation.1 | async-start | bytes 2097152 | tf_op jit(solution)/shard_map/all_to_all | solution.py:245
  144.1 13.6 %all-to-all-done.1 = bf16[16,128,256]{2,1,0:T(8,128)(2,1)S(1)} async-done(((bf16[16,128,256]{2,1,0:T(8,128)(2,1)}), bf16[16,128,256]{2,1,0:T(8,128)(2,1)S(1)}, u32[]{:S(2)}, u32[]{:S(2)}) %all-to-all-start.1) | async-done | bytes 1048608 | tf_op jit(solution)/shard_map/all_to_all | solution.py:245
  157.9 3.4 %collective-permute-start = (f32[128,256]{1,0:T(8,128)S(1)}, f32[128,256]{1,0:T(8,128)S(1)}, u32[]{:S(2)}, u32[]{:S(2)}) collective-permute-start(f32[128,256]{1,0:T(8,128)S(1)} %convert_reduce_fusion), channel_id=1, source_target_pairs={{0,1},{1,0},{2,3},{3,2},{4,5},{5,4},{6,7},{7,6},{8,9},{9,8},{10,11... | collective-permute-start | bytes 393224 | tf_op jit(solution)/shard_map/ppermute | solution.py:251
  161.3 0.6 gather_fusion
  161.9 2.3 %collective-permute-done = f32[128,256]{1,0:T(8,128)S(1)} collective-permute-done((f32[128,256]{1,0:T(8,128)S(1)}, f32[128,256]{1,0:T(8,128)S(1)}, u32[]{:S(2)}, u32[]{:S(2)}) %collective-permute-start) | collective-permute-done | bytes 131104 | tf_op jit(solution)/shard_map/ppermute | solution.py:251
  164.3 1.4 collective-permute-start.1
  165.6 1.2 fusion.7
  167.0 1.1 collective-permute-done.1
  168.2 2.8 %collective-permute-start.2 = (f32[128,256]{1,0:T(8,128)S(1)}, f32[128,256]{1,0:T(8,128)S(1)}, u32[]{:S(2)}, u32[]{:S(2)}) collective-permute-start(f32[128,256]{1,0:T(8,128)S(1)} %add.118), channel_id=1, source_target_pairs={{0,6},{1,7},{2,4},{3,5},{4,2},{5,3},{6,0},{7,1},{8,14},{9,15},{10,... | collective-permute-start | bytes 393224 | tf_op jit(solution)/shard_map/ppermute | solution.py:251
  171.2 2.1 %collective-permute-done.2 = f32[128,256]{1,0:T(8,128)S(1)} collective-permute-done((f32[128,256]{1,0:T(8,128)S(1)}, f32[128,256]{1,0:T(8,128)S(1)}, u32[]{:S(2)}, u32[]{:S(2)}) %collective-permute-start.2) | collective-permute-done | bytes 131104 | tf_op jit(solution)/shard_map/ppermute | solution.py:251
  173.4 8.1 %collective-permute-start.3 = (f32[128,256]{1,0:T(8,128)S(1)}, f32[128,256]{1,0:T(8,128)S(1)}, u32[]{:S(2)}, u32[]{:S(2)}) collective-permute-start(f32[128,256]{1,0:T(8,128)S(1)} %get-tuple-element.6), channel_id=1, source_target_pairs={{0,8},{1,24},{2,40},{3,56},{4,72},{5,88},{6,104},{7,120},{8,0},{9,... | collective-permute-start | bytes 393224 | tf_op jit(solution)/shard_map/ppermute | solution.py:259
  181.6 2.2 %collective-permute-start.4 = (f32[128,256]{1,0:T(8,128)S(1)}, f32[128,256]{1,0:T(8,128)S(1)}, u32[]{:S(2)}, u32[]{:S(2)}) collective-permute-start(f32[128,256]{1,0:T(8,128)S(1)} %get-tuple-element.6), channel_id=1, source_target_pairs={{0,0},{1,16},{2,32},{3,48},{4,64},{5,80},{6,96},{7,112},{8,8},{9,2... | collective-permute-start | bytes 393224 | tf_op jit(solution)/shard_map/ppermute | solution.py:258
  183.8 5.6 %collective-permute-done.3 = f32[128,256]{1,0:T(8,128)S(1)} collective-permute-done((f32[128,256]{1,0:T(8,128)S(1)}, f32[128,256]{1,0:T(8,128)S(1)}, u32[]{:S(2)}, u32[]{:S(2)}) %collective-permute-start.3) | collective-permute-done | bytes 131104 | tf_op jit(solution)/shard_map/ppermute | solution.py:259
  189.4 4.1 %collective-permute-done.4 = f32[128,256]{1,0:T(8,128)S(1)} collective-permute-done((f32[128,256]{1,0:T(8,128)S(1)}, f32[128,256]{1,0:T(8,128)S(1)}, u32[]{:S(2)}, u32[]{:S(2)}) %collective-permute-start.4) | collective-permute-done | bytes 131104 | tf_op jit(solution)/shard_map/ppermute | solution.py:258
  194.2 0.6 convolution_bitcast_fusion
  194.8 1.0 pad_maximum_fusion
  (31 shorter events, 2.0 us)
Async XLA Ops:
  0.0 161.3 %copy-start = (f32[32]{0:T(128)S(1)}, f32[32]{0:T(128)}, u32[]{:S(2)}) copy-start(f32[32]{0:T(128)} %param.11) | copy-start | bytes 388
  13.6 7.8 %copy-start.3 = (s32[3,4096]{1,0:T(4,128)S(1)}, s32[3,4096]{1,0:T(4,128)}, u32[]{:S(2)}) copy-start(s32[3,4096]{1,0:T(4,128)} %param.15) | copy-start | bytes 147460
  13.6 100.3 %copy-start.1 = (bf16[48,384]{1,0:T(8,128)(2,1)S(1)}, bf16[48,384]{1,0:T(8,128)(2,1)}, u32[]{:S(2)}) copy-start(bf16[48,384]{1,0:T(8,128)(2,1)} %constant.95.clone.table_ref) | copy-start | bytes 110596
  13.6 100.3 %copy-start.2 = (s32[2]{0:T(128)S(1)}, s32[2]{0:T(128)}, u32[]{:S(2)}) copy-start(s32[2]{0:T(128)} %own_ref.1) | copy-start | bytes 28
  13.6 100.3 %all-to-all-start = ((bf16[16,3,504,128]{3,2,1,0:T(8,128)(2,1)}), bf16[16,3,504,128]{3,2,1,0:T(8,128)(2,1)}, u32[]{:S(2)}, u32[]{:S(2)}) async-start(bf16[16,3,504,128]{3,2,1,0:T(8,128)(2,1)} %pack.1), calls=%async_computation | async-start | bytes 12386304 | tf_op jit(solution)/shard_map/all_to_all | solution.py:220
  127.1 39.7 %copy-start.4 = (f32[16]{0:T(128)S(1)}, f32[16]{0:T(128)}, u32[]{:S(2)}) copy-start(f32[16]{0:T(128)} %param.12) | copy-start | bytes 196
  136.5 21.2 %all-to-all-start.1 = ((bf16[16,128,256]{2,1,0:T(8,128)(2,1)}), bf16[16,128,256]{2,1,0:T(8,128)(2,1)S(1)}, u32[]{:S(2)}, u32[]{:S(2)}) async-start(bf16[16,128,256]{2,1,0:T(8,128)(2,1)} %gelements.1), calls=%async_computation.1 | async-start | bytes 2097152 | tf_op jit(solution)/shard_map/all_to_all | solution.py:245
  157.9 6.4 %collective-permute-start = (f32[128,256]{1,0:T(8,128)S(1)}, f32[128,256]{1,0:T(8,128)S(1)}, u32[]{:S(2)}, u32[]{:S(2)}) collective-permute-start(f32[128,256]{1,0:T(8,128)S(1)} %convert_reduce_fusion), channel_id=1, source_target_pairs={{0,1},{1,0},{2,3},{3,2},{4,5},{5,4},{6,7},{7,6},{8,9},{9,8},{10,11... | collective-permute-start | bytes 393224 | tf_op jit(solution)/shard_map/ppermute | solution.py:251
  164.3 3.9 %collective-permute-start.1 = (f32[128,256]{1,0:T(8,128)S(1)}, f32[128,256]{1,0:T(8,128)S(1)}, u32[]{:S(2)}, u32[]{:S(2)}) collective-permute-start(f32[128,256]{1,0:T(8,128)S(1)} %add.117), channel_id=1, source_target_pairs={{0,2},{1,3},{2,0},{3,1},{4,6},{5,7},{6,4},{7,5},{8,10},{9,11},{10,... | collective-permute-start | bytes 393224 | tf_op jit(solution)/shard_map/ppermute | solution.py:251
  168.2 5.2 %collective-permute-start.2 = (f32[128,256]{1,0:T(8,128)S(1)}, f32[128,256]{1,0:T(8,128)S(1)}, u32[]{:S(2)}, u32[]{:S(2)}) collective-permute-start(f32[128,256]{1,0:T(8,128)S(1)} %add.118), channel_id=1, source_target_pairs={{0,6},{1,7},{2,4},{3,5},{4,2},{5,3},{6,0},{7,1},{8,14},{9,15},{10,... | collective-permute-start | bytes 393224 | tf_op jit(solution)/shard_map/ppermute | solution.py:251
  173.4 16.0 %collective-permute-start.3 = (f32[128,256]{1,0:T(8,128)S(1)}, f32[128,256]{1,0:T(8,128)S(1)}, u32[]{:S(2)}, u32[]{:S(2)}) collective-permute-start(f32[128,256]{1,0:T(8,128)S(1)} %get-tuple-element.6), channel_id=1, source_target_pairs={{0,8},{1,24},{2,40},{3,56},{4,72},{5,88},{6,104},{7,120},{8,0},{9,... | collective-permute-start | bytes 393224 | tf_op jit(solution)/shard_map/ppermute | solution.py:259
  181.6 12.0 %collective-permute-start.4 = (f32[128,256]{1,0:T(8,128)S(1)}, f32[128,256]{1,0:T(8,128)S(1)}, u32[]{:S(2)}, u32[]{:S(2)}) collective-permute-start(f32[128,256]{1,0:T(8,128)S(1)} %get-tuple-element.6), channel_id=1, source_target_pairs={{0,0},{1,16},{2,32},{3,48},{4,64},{5,80},{6,96},{7,112},{8,8},{9,2... | collective-permute-start | bytes 393224 | tf_op jit(solution)/shard_map/ppermute | solution.py:258
